TPU v7x, 256 devices: a whole 4x4x8 slice. The times are simulated.
256 devices in a mesh: docs: 64 (over x, z, core), terms: 4 (over y).
Axes of the slice: x: 4, y: 4, z: 8, core: 2. Of those that a mesh axis runs over, the one named last changes fastest.
Arguments:
- values: bfloat16 [256, 64, 64, 128], P('docs', 'terms')
- block_ids: int32 [256, 64], P('docs', 'terms'), may hold values from 0 to 2047, as said below
- assignment: int32 [16384, 1], P('docs'), may hold values from 0 to 511
Outputs:
- coefficients: float32 [16384, 512], P('docs', 'terms')
Inputs may be any that keep to these rules, and one draw needn't show every extreme that they name: `assignment`: every one of the 512 clusters has at least one document. `block_ids`: in each term slice, the 16 blocks of one tile lie in 16 different ranges of 32 consecutive block numbers, and the tiles of one index of docs place exactly 1 block in each such range.
All inputs are finite; a program needn't handle non-finite values.
Results may differ from a plain program's by a relative error of at most 0.00045.
Values may be sent and summed in bfloat16 or wider, within the bound.
A program may use at most 128 MiB of HBM per device.

v0:
```python
import jax
import jax.numpy as jnp
from jax import lax
from jax.sharding import PartitionSpec as P

K = 512
BLK_OWN = 32
EPSILON = 1e-06
RIDGE_WEIGHT = 1.0


def send_order(owner, capacity):
    pairs = owner.shape[0]
    counter = jnp.arange(pairs, dtype=jnp.int32)
    same = owner[:, None] == owner[None, :]
    earlier = counter[None, :] < counter[:, None]
    rank = jnp.sum((same & earlier).astype(jnp.int32), axis=1)
    target = owner * capacity + rank
    source = jnp.zeros((pairs,), jnp.int32).at[target].set(counter)
    return (target, source)


def pick_tile(labels, tile_index):
    return labels[tile_index]


def body(values, block_ids, assignment):
    tiles_here, slot_count, tile_rows, block_width = values.shape
    peers = lax.axis_size("docs")
    pairs = tiles_here * slot_count
    capacity = pairs // peers
    arrivals = peers * capacity
    doc_rows = tiles_here * tile_rows
    all_blocks, all_labels = (
        lax.all_gather(block_ids, "docs", axis=0, tiled=True),
        lax.all_gather(assignment, "docs", axis=0, tiled=True),
    )
    own_target, own_source = send_order((block_ids // BLK_OWN).reshape(pairs), capacity)
    flat_values = values.reshape(pairs, tile_rows, block_width)
    outgoing = flat_values[own_source].reshape(peers, capacity, tile_rows, block_width)
    arrived = lax.all_to_all(outgoing, "docs", split_axis=0, concat_axis=0, tiled=True)
    arrived = arrived.reshape(arrivals, tile_rows, block_width)
    sender_blocks = all_blocks.reshape(peers, pairs)

    def sender_source(blocks):
        return send_order(blocks // BLK_OWN, capacity)[1]

    sender_sources = jax.vmap(sender_source)(sender_blocks)
    mine = lax.dynamic_slice_in_dim(sender_sources, lax.axis_index("docs") * capacity, capacity, 1)
    local_block = (jnp.take_along_axis(sender_blocks, mine, axis=1) % BLK_OWN).reshape(arrivals)
    tile_of = mine // slot_count
    sender_labels = all_labels[:, 0].reshape(peers, tiles_here, tile_rows)
    arrived_labels = jax.vmap(pick_tile)(sender_labels, tile_of).reshape(arrivals, tile_rows)
    cluster_hot = (
        arrived_labels[:, :, None] == jnp.arange(K, dtype=jnp.int32)[None, None, :]
    ).astype(jnp.bfloat16)
    contrib = jnp.einsum("rtk,rtb->rkb", cluster_hot, arrived, preferred_element_type=jnp.float32)
    block_hot = (local_block[:, None] == jnp.arange(BLK_OWN, dtype=jnp.int32)[None, :]).astype(
        jnp.float32
    )
    sums_own = jnp.einsum(
        "rc,rkb->kcb",
        block_hot,
        contrib,
        precision=lax.Precision.HIGHEST,
        preferred_element_type=jnp.float32,
    )
    sums_own = sums_own.reshape(K, BLK_OWN * block_width)
    sq_total = lax.psum(jnp.sum(sums_own * sums_own, axis=1), ("docs", "terms"))
    concepts_own = (sums_own * lax.rsqrt(sq_total + EPSILON)[:, None]).astype(jnp.bfloat16)
    gram_part = jnp.dot(concepts_own, concepts_own.T, preferred_element_type=jnp.float32)
    gram_matrix = lax.psum(gram_part, ("docs", "terms"))
    identity = jnp.eye(K, dtype=jnp.float32)
    factor = jnp.linalg.cholesky(gram_matrix + RIDGE_WEIGHT * identity)
    inverse = jax.scipy.linalg.cho_solve((factor, True), identity)
    concept_blocks = jnp.transpose(concepts_own.reshape(K, BLK_OWN, block_width), (1, 0, 2))
    wanted = concept_blocks[local_block]
    reply = lax.all_to_all(
        wanted.reshape(peers, capacity, K, block_width),
        "docs",
        split_axis=0,
        concat_axis=0,
        tiled=True,
    )
    fetched = reply.reshape(pairs, K, block_width)[own_target].reshape(
        tiles_here, slot_count, K, block_width
    )
    scores_part = jnp.einsum("isrb,iskb->irk", values, fetched, preferred_element_type=jnp.float32)
    scores_part = scores_part.reshape(doc_rows, K)
    col_width = K // lax.axis_size("terms")
    scores = lax.psum(scores_part, "terms")
    inverse_cols = lax.dynamic_slice_in_dim(
        inverse, lax.axis_index("terms") * col_width, col_width, 1
    )
    return jnp.dot(
        scores, inverse_cols, precision=lax.Precision.HIGHEST, preferred_element_type=jnp.float32
    )


def solution(mesh):
    in_specs = (P("docs", "terms", None, None), P("docs", "terms"), P("docs", None))
    out_specs = P("docs", "terms")
    return jax.shard_map(body, mesh=mesh, in_specs=in_specs, out_specs=out_specs, check_vma=False)
```

profile of v0, /device:TPU:2, one launch (start us, length us, event | category | flops | bytes accessed | tf_op | source)
XLA Modules:
  0.0 813.5 jit_solution(112224903261461516)
XLA Ops:
  11.2 12.0 %all-to-all-start = ((bf16[64,1,64,128]{3,2,1,0:T(8,128)(2,1)}), bf16[64,1,64,128]{3,2,1,0:T(8,128)(2,1)S(1)}, u32[]{:S(2)}, u32[]{:S(2)}) async-start(bf16[64,1,64,128]{3,2,1,0:T(8,128)(2,1)} %bitcast.7), calls=%async_computation | async-start | bytes 2097152 | tf_op jit(solution)/shard_map/all_to_all | solution.py:41
  23.3 67.7 %all-gather = s32[64,4,16]{2,1,0:T(4,128)S(1)} all-gather(s32[1,4,16]{2,1,0:T(4,128)} %bitcast.108), channel_id=1, replica_groups=mesh['docs'=64,'terms'=4] {'docs'}, dimensions={0}, use_global_device_ids=true | all-gather | bytes 16640 | tf_op jit(solution)/shard_map/all_gather | solution.py:35
  94.1 15.5 %scatter_custom_fusion.1 = s32[4096]{0:T(1024)S(1)} fusion(s32[4096]{0:T(1024)S(1)} %reshape.365, s32[4096]{0:T(1024)S(1)} %reshape.367, s32[]{:T(128)} %copy.156), kind=kCustom, calls=%fused_computation.147 | custom fusion | bytes 16388
  110.1 41.3 %all_gather.6 = s32[16384,1]{0,1:T(1,128)S(1)} all-gather(s32[256,1]{0,1:T(1,128)} %param.5), channel_id=1, replica_groups=mesh['docs'=64,'terms'=4] {'docs'}, dimensions={0}, use_global_device_ids=true | all-gather | bytes 66560 | tf_op jit(solution)/shard_map/all_gather | solution.py:36
  155.3 5.5 fusion.2
  160.8 26.4 %multiply_reduce_fusion = (f32[512]{0:T(512)S(1)}, f32[512,128,32]{1,2,0:T(8,128)}) fusion(s32[64]{0:T(128)S(1)} %get-tuple-element.14, f32[64,512,128]{2,1,0:T(8,128)S(1)} %fusion.2), kind=kOutput, calls=%fused_computation.12 | convolution fusion | flops 1614808576 | bytes 25168128 | tf_op jit(solution)/shard_map/rc,rkb->kcb/dot_general | solution.py:61
  187.2 77.1 %psum.21 = f32[512]{0:T(512)S(1)} all-reduce(f32[512]{0:T(512)S(1)} %get-tuple-element.45), channel_id=1, replica_groups=mesh['docs'=64,'terms'=4] {'docs','terms'}, use_global_device_ids=true, to_apply=%region_5.6 | all-reduce | flops 512 | bytes 4096 | tf_op jit(solution)/shard_map/psum | solution.py:69
  264.3 5.6 fusion.88
  269.9 3.5 copy.113
  273.4 7.7 gather_fusion.1
  281.1 9.2 %all-to-all-start.1 = ((bf16[64,1,512,128]{3,2,1,0:T(8,128)(2,1)}), bf16[64,1,512,128]{3,2,1,0:T(8,128)(2,1)}, u32[]{:S(2)}, u32[]{:S(2)}) async-start(bf16[64,1,512,128]{3,2,1,0:T(8,128)(2,1)} %bitcast.103), calls=%async_computation.1 | async-start | bytes 16777216 | tf_op jit(solution)/shard_map/all_to_all | solution.py:78
  290.4 6.9 fusion.6
  299.5 293.0 %all-reduce.6.cloned.1.call-done = f32[512,512]{0,1:T(8,128)} async-done(((f32[512,512]{0,1:T(8,128)}), f32[512,512]{0,1:T(8,128)}) %all-reduce.6.cloned.1.call-update) | async-done | bytes 1048592 | tf_op jit(solution)/shard_map/psum | solution.py:72
  595.7 11.7 %cholesky.104 = f32[128,128]{1,0:T(8,128)S(1)} custom-call(f32[128,128]{1,0:T(8,128)S(1)} %cholesky.266), custom_call_target="Cholesky" | custom-call | tf_op jit(solution)/shard_map/jit(cholesky)/cholesky | solution.py:74
  607.5 9.8 %custom-call.34 = f32[1,128,128]{1,2,0:T(8,128)S(1)} custom-call(f32[1,128,128]{2,1,0:T(8,128)S(1)} %get-tuple-element.38), custom_call_target="InvertDiagBlocksLowerTriangular" | custom-call | tf_op jit(solution)/shard_map/jit(cholesky)/cholesky | solution.py:74
  618.0 11.7 %cholesky.217 = f32[128,128]{1,0:T(8,128)S(1)} custom-call(f32[128,128]{1,0:T(8,128)S(1)} %cholesky.270), custom_call_target="Cholesky" | custom-call | tf_op jit(solution)/shard_map/jit(cholesky)/cholesky | solution.py:74
  629.8 10.0 %custom-call.35 = f32[1,128,128]{1,2,0:T(8,128)S(1)} custom-call(f32[1,128,128]{2,1,0:T(8,128)S(1)} %get-tuple-element.35), custom_call_target="InvertDiagBlocksLowerTriangular" | custom-call | tf_op jit(solution)/shard_map/jit(cholesky)/cholesky | solution.py:74
  640.4 11.7 %cholesky.238 = f32[128,128]{1,0:T(8,128)S(1)} custom-call(f32[128,128]{1,0:T(8,128)S(1)} %cholesky.275), custom_call_target="Cholesky" | custom-call | tf_op jit(solution)/shard_map/jit(cholesky)/cholesky | solution.py:74
  652.2 9.8 %custom-call.36 = f32[1,128,128]{1,2,0:T(8,128)S(1)} custom-call(f32[1,128,128]{2,1,0:T(8,128)S(1)} %get-tuple-element.32), custom_call_target="InvertDiagBlocksLowerTriangular" | custom-call | tf_op jit(solution)/shard_map/jit(cholesky)/cholesky | solution.py:74
  662.6 11.7 %cholesky.255 = f32[128,128]{1,0:T(8,128)S(1)} custom-call(f32[128,128]{1,0:T(8,128)S(1)} %convolution_subtract_fusion.8), custom_call_target="Cholesky" | custom-call | tf_op jit(solution)/shard_map/jit(cholesky)/cholesky | solution.py:74
  679.9 10.5 %while.1 = (s32[]{:T(128)}, f32[512,512]{1,0:T(8,128)S(1)}, s32[4,2]{0,1:T(2,128)S(1)}, f32[4,128,128]{2,1,0:T(8,128)}, s32[]{:T(128)}) while((s32[]{:T(128)}, f32[512,512]{1,0:T(8,128)S(1)}, s32[4,2]{0,1:T(2,128)S(1)}, f32[4,128,128]{2,1,0:T(8,128)}, s32[]{:T(128)}) %tuple.35), condition=%wide.while_cond, body=%wide.while_body.sunk | while | flops 2 | bytes 132705 | solution.py:75
  680.6 2.0 bitcast_dynamic-update-slice_fusion.2
  683.2 2.0 bitcast_dynamic-update-slice_fusion.2
  685.8 2.0 bitcast_dynamic-update-slice_fusion.2
  688.5 2.0 bitcast_dynamic-update-slice_fusion.2
  690.4 40.1 %custom-call.37 = f32[4,128,128]{1,2,0:T(8,128)S(1)} custom-call(f32[4,128,128]{2,1,0:T(8,128)} %get-tuple-element.12), custom_call_target="InvertDiagBlocksLowerTriangular" | custom-call | tf_op jit(solution)/shard_map/jit(_cho_solve)/triangular_solve | solution.py:75
  733.6 1.9 convolution_subtract_fusion.2
  736.0 2.4 convolution_subtract_fusion.5
  741.2 8.9 %gather_fusion.2 = bf16[64,512,128]{2,1,0:T(8,128)(2,1)} fusion(bf16[64,512,128]{2,1,0:T(8,128)(2,1)} %bitcast.15, s32[1024]{0:T(1024)S(1)} %pad_clamp_fusion), kind=kCustom, calls=%fused_computation.2 | custom fusion | bytes 16777472 | tf_op jit(solution)/shard_map/gather | solution.py:85
  750.1 6.8 fusion.93
  759.3 44.3 %all-reduce.4.cloned.1.call-done = f32[256,512]{1,0:T(8,128)} async-done(((f32[256,512]{1,0:T(8,128)}), f32[256,512]{1,0:T(8,128)}) %all-reduce.4.cloned.1.call-update) | async-done | bytes 524304 | tf_op jit(solution)/shard_map/psum | solution.py:91
  803.6 2.3 fusion.31
  (101 shorter events, 33.1 us)
Async XLA Ops:
  7.4 2.2 copy-start
  11.2 144.1 %all-to-all-start = ((bf16[64,1,64,128]{3,2,1,0:T(8,128)(2,1)}), bf16[64,1,64,128]{3,2,1,0:T(8,128)(2,1)S(1)}, u32[]{:S(2)}, u32[]{:S(2)}) async-start(bf16[64,1,64,128]{3,2,1,0:T(8,128)(2,1)} %bitcast.7), calls=%async_computation | async-start | bytes 2097152 | tf_op jit(solution)/shard_map/all_to_all | solution.py:41
  281.1 460.0 %all-to-all-start.1 = ((bf16[64,1,512,128]{3,2,1,0:T(8,128)(2,1)}), bf16[64,1,512,128]{3,2,1,0:T(8,128)(2,1)}, u32[]{:S(2)}, u32[]{:S(2)}) async-start(bf16[64,1,512,128]{3,2,1,0:T(8,128)(2,1)} %bitcast.103), calls=%async_computation.1 | async-start | bytes 16777216 | tf_op jit(solution)/shard_map/all_to_all | solution.py:78
  290.4 302.2 %all-reduce.6.cloned.1.call-start = ((), (), s32[]{:S(2)}) async-start(), calls=%async_computation.3 | async-start | bytes 2097152 | tf_op jit(solution)/shard_map/psum | solution.py:72
  297.3 506.3 %all-reduce.4.cloned.1.call-start = ((), (), s32[]{:S(2)}) async-start(), calls=%async_computation.2 | async-start | bytes 1048576 | tf_op jit(solution)/shard_map/psum | solution.py:91
Sparse Core Ops, SparseCore 0:
  297.4 295.0 all-reduce.5
Sparse Core Ops, SparseCore 1:
  757.0 46.6 all-reduce.3
where the time goes:
time: 821 us; the launch traced here: 813 us
  waiting for transfers between devices  337 us (41%)
  blocking collectives  186 us (23%)
  other arithmetic  135 us (16%)
  matrix products  62.6 us (8%)
  local copies, waits for them, and re-layouts  52.6 us (6%)
  starting transfers between devices  21.5 us (3%)
  between operations  17.9 us (2%)
    psum x1, waiting for transfers between devices, body(): gram_matrix = lax.psum(gram_part, ('docs', 'terms'))  293 us
    another operation x15, other arithmetic, body(): factor = jnp.linalg.cholesky(gram_matrix + RIDGE_WEIGHT * identity)  79.6 us
    psum x1, blocking collectives, body(): sq_total = lax.psum(jnp.sum(sums_own * sums_own, axis=1), ('docs', 'terms'))  77.1 us
    all_gather x1, blocking collectives, body(): lax.all_gather(block_ids, 'docs', axis=0, tiled=True)  67.7 us
    psum x1, waiting for transfers between devices, body(): scores = lax.psum(scores_part, 'terms')  44.3 us
    all_gather x1, blocking collectives, body(): lax.all_gather(assignment, 'docs', axis=0, tiled=True)  41.3 us
    another operation x3, other arithmetic, body(): inverse = jax.scipy.linalg.cho_solve((factor, True), identity)  40.3 us
    dot_general x1, matrix products, body(): jnp.einsum('rc,rkb->kcb', block_hot, contrib, precision=lax.Precision.HIG...  26.4 us
  transfers between devices with their start and end apart: 4, of which 2 were waited for; matrix products, arithmetic and copies ran while one was open for 22% of the time, Pallas kernels for 0%

commit v1 on v0

--- a/solution.py
+++ b/solution.py
@@ -7,6 +7,19 @@
 BLK_OWN = 32
 EPSILON = 1e-06
 RIDGE_WEIGHT = 1.0
+
+
+def _push_table(block_here):
+    taken_in = jnp.concatenate(
+        lax.all_to_all(
+            jnp.stack(tuple((block_here for _ in range(lax.axis_size("docs"))))),
+            axis_name="docs",
+            split_axis=0,
+            concat_axis=0,
+        ),
+        axis=0,
+    )
+    return taken_in
 
 
 def send_order(owner, capacity):
@@ -33,7 +46,7 @@
     doc_rows = tiles_here * tile_rows
     all_blocks, all_labels = (
         lax.all_gather(block_ids, "docs", axis=0, tiled=True),
-        lax.all_gather(assignment, "docs", axis=0, tiled=True),
+        _push_table(assignment),
     )
     own_target, own_source = send_order((block_ids // BLK_OWN).reshape(pairs), capacity)
     flat_values = values.reshape(pairs, tile_rows, block_width)

time: 821 us -> 790 us (0.962)
  blocking collectives: 186 us -> 145 us
    all_gather x1 -> x0, blocking collectives: 41.3 us -> none  [body(): lax.all_gather(assignment, 'docs', axis=0, tiled=True)]
    all_to_all x0 -> x1, starting transfers between devices: none -> 12 us  [_push_table(): lax.all_to_all(jnp.stack(tuple((block_here for _ in range(lax.axis_size('...]
  transfers between devices with their start and end apart: 4 -> 5, of which waited for: 2 -> 3; matrix products, arithmetic and copies ran while one was open for 22% -> 23% of each run, Pallas kernels for 0% -> 0%
where the time goes in v1:
time: 790 us; the launch traced here: 782 us
  waiting for transfers between devices  343 us (43%)
  blocking collectives  145 us (18%)
  other arithmetic  135 us (17%)
  matrix products  62.6 us (8%)
  local copies, waits for them, and re-layouts  53 us (7%)
  starting transfers between devices  26.1 us (3%)
  between operations  18 us (2%)
    psum x1, waiting for transfers between devices, body(): gram_matrix = lax.psum(gram_part, ('docs', 'terms'))  294 us
    another operation x15, other arithmetic, body(): factor = jnp.linalg.cholesky(gram_matrix + RIDGE_WEIGHT * identity)  79.5 us
    psum x1, blocking collectives, body(): sq_total = lax.psum(jnp.sum(sums_own * sums_own, axis=1), ('docs', 'terms'))  77.2 us
    all_gather x1, blocking collectives, body(): lax.all_gather(block_ids, 'docs', axis=0, tiled=True)  67.7 us
    psum x1, waiting for transfers between devices, body(): scores = lax.psum(scores_part, 'terms')  44.3 us
    another operation x3, other arithmetic, body(): inverse = jax.scipy.linalg.cho_solve((factor, True), identity)  40.3 us
    dot_general x1, matrix products, body(): jnp.einsum('rc,rkb->kcb', block_hot, contrib, precision=lax.Precision.HIG...  26.4 us
    unnamed x10, local copies, waits for them, and re-layouts  16 us
  transfers between devices with their start and end apart: 5, of which 3 were waited for; matrix products, arithmetic and copies ran while one was open for 23% of the time, Pallas kernels for 0%

profile of v1, /device:TPU:2, one launch (start us, length us, event | category | flops | bytes accessed | tf_op | source)
XLA Modules:
  0.0 782.1 jit_solution(15097769837618460364)
XLA Ops:
  8.8 12.0 %all-to-all-start = ((s32[64,256,1]{1,2,0:T(1,128)}), s32[64,256,1]{1,2,0:T(1,128)S(1)}, u32[]{:S(2)}, u32[]{:S(2)}) async-start(s32[64,256,1]{1,2,0:T(1,128)} %stack.2), calls=%async_computation | async-start | bytes 131072 | tf_op jit(solution)/shard_map/all_to_all | solution.py:14
  24.6 5.1 all-to-all-done
  29.7 5.5 all-to-all-start.1
  35.2 67.7 %all-gather = s32[64,4,16]{2,1,0:T(4,128)S(1)} all-gather(s32[1,4,16]{2,1,0:T(4,128)} %bitcast.108), channel_id=1, replica_groups=mesh['docs'=64,'terms'=4] {'docs'}, dimensions={0}, use_global_device_ids=true | all-gather | bytes 16640 | tf_op jit(solution)/shard_map/all_gather | solution.py:48
  106.1 15.5 %scatter_custom_fusion.1 = s32[4096]{0:T(1024)S(1)} fusion(s32[4096]{0:T(1024)S(1)} %reshape.368, s32[4096]{0:T(1024)S(1)} %reshape.370, s32[]{:T(128)} %copy.156), kind=kCustom, calls=%fused_computation.147 | custom fusion | bytes 16388
  124.7 5.5 fusion.2
  130.2 26.4 %multiply_reduce_fusion = (f32[512]{0:T(512)S(1)}, f32[512,128,32]{1,2,0:T(8,128)}) fusion(s32[64]{0:T(128)S(1)} %get-tuple-element.14, f32[64,512,128]{2,1,0:T(8,128)S(1)} %fusion.2), kind=kOutput, calls=%fused_computation.12 | convolution fusion | flops 1614808576 | bytes 25168128 | tf_op jit(solution)/shard_map/rc,rkb->kcb/dot_general | solution.py:74
  156.6 77.2 %psum.21 = f32[512]{0:T(512)S(1)} all-reduce(f32[512]{0:T(512)S(1)} %get-tuple-element.45), channel_id=1, replica_groups=mesh['docs'=64,'terms'=4] {'docs','terms'}, use_global_device_ids=true, to_apply=%region_5.6 | all-reduce | flops 512 | bytes 4096 | tf_op jit(solution)/shard_map/psum | solution.py:82
  233.8 5.6 fusion.88
  239.4 3.5 copy.113
  242.9 7.7 gather_fusion.1
  250.6 8.3 %all-to-all-start.2 = ((bf16[64,1,512,128]{3,2,1,0:T(8,128)(2,1)}), bf16[64,1,512,128]{3,2,1,0:T(8,128)(2,1)}, u32[]{:S(2)}, u32[]{:S(2)}) async-start(bf16[64,1,512,128]{3,2,1,0:T(8,128)(2,1)} %bitcast.103), calls=%async_computation.2 | async-start | bytes 16777216 | tf_op jit(solution)/shard_map/all_to_all | solution.py:91
  258.9 6.9 fusion.6
  268.0 293.6 %all-reduce.6.cloned.1.call-done = f32[512,512]{0,1:T(8,128)} async-done(((f32[512,512]{0,1:T(8,128)}), f32[512,512]{0,1:T(8,128)}) %all-reduce.6.cloned.1.call-update) | async-done | bytes 1048592 | tf_op jit(solution)/shard_map/psum | solution.py:85
  564.7 11.7 %cholesky.104 = f32[128,128]{1,0:T(8,128)S(1)} custom-call(f32[128,128]{1,0:T(8,128)S(1)} %cholesky.266), custom_call_target="Cholesky" | custom-call | tf_op jit(solution)/shard_map/jit(cholesky)/cholesky | solution.py:87
  576.6 9.8 %custom-call.34 = f32[1,128,128]{1,2,0:T(8,128)S(1)} custom-call(f32[1,128,128]{2,1,0:T(8,128)S(1)} %get-tuple-element.38), custom_call_target="InvertDiagBlocksLowerTriangular" | custom-call | tf_op jit(solution)/shard_map/jit(cholesky)/cholesky | solution.py:87
  587.1 11.7 %cholesky.217 = f32[128,128]{1,0:T(8,128)S(1)} custom-call(f32[128,128]{1,0:T(8,128)S(1)} %cholesky.270), custom_call_target="Cholesky" | custom-call | tf_op jit(solution)/shard_map/jit(cholesky)/cholesky | solution.py:87
  598.8 10.0 %custom-call.35 = f32[1,128,128]{1,2,0:T(8,128)S(1)} custom-call(f32[1,128,128]{2,1,0:T(8,128)S(1)} %get-tuple-element.35), custom_call_target="InvertDiagBlocksLowerTriangular" | custom-call | tf_op jit(solution)/shard_map/jit(cholesky)/cholesky | solution.py:87
  609.5 11.7 %cholesky.238 = f32[128,128]{1,0:T(8,128)S(1)} custom-call(f32[128,128]{1,0:T(8,128)S(1)} %cholesky.275), custom_call_target="Cholesky" | custom-call | tf_op jit(solution)/shard_map/jit(cholesky)/cholesky | solution.py:87
  621.3 9.8 %custom-call.36 = f32[1,128,128]{1,2,0:T(8,128)S(1)} custom-call(f32[1,128,128]{2,1,0:T(8,128)S(1)} %get-tuple-element.32), custom_call_target="InvertDiagBlocksLowerTriangular" | custom-call | tf_op jit(solution)/shard_map/jit(cholesky)/cholesky | solution.py:87
  631.7 11.7 %cholesky.255 = f32[128,128]{1,0:T(8,128)S(1)} custom-call(f32[128,128]{1,0:T(8,128)S(1)} %convolution_subtract_fusion.8), custom_call_target="Cholesky" | custom-call | tf_op jit(solution)/shard_map/jit(cholesky)/cholesky | solution.py:87
  649.0 10.1 %while.1 = (s32[]{:T(128)}, f32[512,512]{1,0:T(8,128)S(1)}, s32[4,2]{0,1:T(2,128)S(1)}, f32[4,128,128]{2,1,0:T(8,128)}, s32[]{:T(128)}) while((s32[]{:T(128)}, f32[512,512]{1,0:T(8,128)S(1)}, s32[4,2]{0,1:T(2,128)S(1)}, f32[4,128,128]{2,1,0:T(8,128)}, s32[]{:T(128)}) %tuple.35), condition=%wide.while_cond, body=%wide.while_body.sunk | while | flops 2 | bytes 132705 | solution.py:88
  649.6 1.9 bitcast_dynamic-update-slice_fusion.2
  652.1 1.9 bitcast_dynamic-update-slice_fusion.2
  654.7 1.9 bitcast_dynamic-update-slice_fusion.2
  659.1 40.1 %custom-call.37 = f32[4,128,128]{1,2,0:T(8,128)S(1)} custom-call(f32[4,128,128]{2,1,0:T(8,128)} %get-tuple-element.12), custom_call_target="InvertDiagBlocksLowerTriangular" | custom-call | tf_op jit(solution)/shard_map/jit(_cho_solve)/triangular_solve | solution.py:88
  702.3 1.9 convolution_subtract_fusion.2
  704.7 2.4 convolution_subtract_fusion.5
  709.8 8.9 %gather_fusion.2 = bf16[64,512,128]{2,1,0:T(8,128)(2,1)} fusion(bf16[64,512,128]{2,1,0:T(8,128)(2,1)} %bitcast.16, s32[1024]{0:T(1024)S(1)} %pad_clamp_fusion), kind=kCustom, calls=%fused_computation.2 | custom fusion | bytes 16777472 | tf_op jit(solution)/shard_map/gather | solution.py:98
  718.7 6.8 fusion.93
  727.9 44.3 %all-reduce.4.cloned.1.call-done = f32[256,512]{1,0:T(8,128)} async-done(((f32[256,512]{1,0:T(8,128)}), f32[256,512]{1,0:T(8,128)}) %all-reduce.4.cloned.1.call-update) | async-done | bytes 524304 | tf_op jit(solution)/shard_map/psum | solution.py:104
  772.3 2.3 fusion.31
  (102 shorter events, 34.7 us)
Async XLA Ops:
  7.4 15.5 %copy-start = (bf16[4,16,64,128]{3,2,1,0:T(8,128)(2,1)S(1)}, bf16[4,16,64,128]{3,2,1,0:T(8,128)(2,1)}, u32[]{:S(2)}) copy-start(bf16[4,16,64,128]{3,2,1,0:T(8,128)(2,1)} %param.3) | copy-start | bytes 3145732
  8.8 20.9 %all-to-all-start = ((s32[64,256,1]{1,2,0:T(1,128)}), s32[64,256,1]{1,2,0:T(1,128)S(1)}, u32[]{:S(2)}, u32[]{:S(2)}) async-start(s32[64,256,1]{1,2,0:T(1,128)} %stack.2), calls=%async_computation | async-start | bytes 131072 | tf_op jit(solution)/shard_map/all_to_all | solution.py:14
  29.7 95.0 %all-to-all-start.1 = ((bf16[64,1,64,128]{3,2,1,0:T(8,128)(2,1)}), bf16[64,1,64,128]{3,2,1,0:T(8,128)(2,1)S(1)}, u32[]{:S(2)}, u32[]{:S(2)}) async-start(bf16[64,1,64,128]{3,2,1,0:T(8,128)(2,1)} %bitcast.8), calls=%async_computation.1 | async-start | bytes 2097152 | tf_op jit(solution)/shard_map/all_to_all | solution.py:54
  250.6 459.2 %all-to-all-start.2 = ((bf16[64,1,512,128]{3,2,1,0:T(8,128)(2,1)}), bf16[64,1,512,128]{3,2,1,0:T(8,128)(2,1)}, u32[]{:S(2)}, u32[]{:S(2)}) async-start(bf16[64,1,512,128]{3,2,1,0:T(8,128)(2,1)} %bitcast.103), calls=%async_computation.2 | async-start | bytes 16777216 | tf_op jit(solution)/shard_map/all_to_all | solution.py:91
  258.9 302.7 %all-reduce.6.cloned.1.call-start = ((), (), s32[]{:S(2)}) async-start(), calls=%async_computation.4 | async-start | bytes 2097152 | tf_op jit(solution)/shard_map/psum | solution.py:85
  265.8 506.4 %all-reduce.4.cloned.1.call-start = ((), (), s32[]{:S(2)}) async-start(), calls=%async_computation.3 | async-start | bytes 1048576 | tf_op jit(solution)/shard_map/psum | solution.py:104
Sparse Core Ops, SparseCore 0:
  266.0 295.5 all-reduce.5
Sparse Core Ops, SparseCore 1:
  725.6 46.6 all-reduce.3
